TPU v7x, 32 devices: a whole 2x2x4 slice. The times are simulated.
32 devices in a mesh: gx: 8 (over y, x, core), gy: 4 (over z).
Axes of the slice: x: 2, y: 2, z: 4, core: 2. Of those that a mesh axis runs over, the one named last changes fastest.
Arguments:
- support_funcs: bfloat16 [3072, 16, 128], P('gx', 'gy'), may hold values from -6 to 6
- potential: float32 [16, 128], P('gy'), may hold values from -1 to 1
- kernel: bfloat16 [4, 48, 64, 64], P('gy', 'gx'), may hold values from -0.375 to 0.375
- weighted: bfloat16 [4, 48, 64, 64], P('gy', 'gx'), may hold values from -0.375 to 0.375
- columns: int32 [48, 4], P('gx'), may hold values from 0 to 47, as said below
- regions: int32 [48, 4], P('gx'), may hold values from 0 to 128, as said below
Outputs:
- new_support: float32 [3072, 16, 128], P('gx', 'gy')
- hamiltonian: float32 [4, 48, 64, 64], P('gy', 'gx')
Inputs may be any that keep to these rules, and one draw needn't show every extreme that they name: `columns`: the column blocks of row block a are 4 distinct blocks among the 18 blocks owned by gx index a // 6 and its two neighbours, counted cyclically. `regions`: every box spans at least half of 16 along y and half of 128 along z; it starts at 0 in both dimensions where the block index is even and ends at 16 and 128 where it is odd.
All inputs are finite; a program needn't handle non-finite values.
Results may differ from a plain program's by a relative error of at most 0.0011.
Values may be sent and summed in bfloat16 or wider, within the bound.
A program may use at most 64 MiB of HBM per device.

v0:
```python
import jax
import jax.numpy as jnp
from jax import lax
from jax.sharding import PartitionSpec as P

SWEEPS = 3


kinetic_cut = 1.0
step_length = 0.5


def with_halo(array, sides, width, wrap):
    for axis, dim in sides:
        peers, length = (lax.axis_size(axis), array.shape[dim])
        up = [(i, (i + 1) % peers) for i in range(peers if wrap else peers - 1)]
        down = [(j, i) for i, j in up]
        last = lax.slice_in_dim(array, length - width, length, axis=dim)
        leading = lax.slice_in_dim(array, 0, width, axis=dim)
        before = lax.ppermute(last, axis, up)
        after = lax.ppermute(leading, axis, down)
        array = jnp.concatenate([before, array, after], axis=dim)
    return array


def apply_ham(widened, potential):
    center = widened[:, 1:-1].astype(jnp.float32)
    beside = (
        widened[:, 2:].astype(jnp.float32)
        + widened[:, :-2].astype(jnp.float32)
        + jnp.roll(center, 1, 2)
        + jnp.roll(center, -1, 2)
    )
    return -0.5 * (beside - 4.0 * center) + potential[None] * center


def local(support_funcs, potential, kernel, weighted, columns, regions):
    block_count = columns.shape[0]
    block_size = kernel.shape[2]
    orbitals = support_funcs.shape[0]
    rows_y = support_funcs.shape[1]
    depth_z = support_funcs.shape[2]
    cells = rows_y * depth_z
    owner_count = lax.axis_size("gx")
    owner_index = lax.axis_index("gx")
    total_y = rows_y * lax.axis_size("gy")
    widened = with_halo(support_funcs, (("gy", 1),), 1, False)
    applied = apply_ham(widened, potential).astype(jnp.bfloat16)
    stacked = with_halo(jnp.stack([support_funcs, applied]), (("gx", 1),), orbitals, True)
    phi_near = stacked[0]
    applied_near = stacked[1]
    slot_count = 3 * block_count
    owner_of = columns // block_count
    relative = (owner_of - owner_index + 1 + owner_count) % owner_count
    position = relative * block_count + columns % block_count
    selector = (
        position[:, :, None] == jnp.arange(slot_count, dtype=jnp.int32)[None, None, :]
    ).astype(jnp.bfloat16)
    picks = selector
    kern_part = jnp.einsum(
        "akc,kaij->aicj",
        picks,
        lax.all_gather(kernel, "gy", axis=0, tiled=True),
        preferred_element_type=jnp.float32,
    )
    wght_part = jnp.einsum(
        "akc,kaij->aicj",
        picks,
        lax.all_gather(weighted, "gy", axis=0, tiled=True),
        preferred_element_type=jnp.float32,
    )
    mixing = jnp.concatenate(
        [kern_part.reshape(orbitals, 3 * orbitals), -wght_part.reshape(orbitals, 3 * orbitals)],
        axis=1,
    ).astype(jnp.bfloat16)
    sources = jnp.concatenate([applied_near, phi_near], axis=0).reshape(6 * orbitals, cells)
    gradient = jnp.dot(mixing, sources, preferred_element_type=jnp.float32).reshape(
        orbitals, rows_y, depth_z
    )
    volume = 1.0 / (total_y * depth_z)
    intersections = (
        lax.dot_general(
            support_funcs.reshape(orbitals, cells),
            applied_near.reshape(3 * orbitals, cells),
            (((1,), (1,)), ((), ())),
            preferred_element_type=jnp.float32,
        )
        * volume
    )
    blocked = intersections.reshape(block_count, block_size, slot_count, block_size)
    picks = selector.astype(jnp.float32)
    hamiltonian = lax.psum_scatter(
        jnp.einsum("akc,aicj->kaij", picks, blocked, precision=lax.Precision.HIGHEST),
        "gy",
        scatter_dimension=0,
        tiled=True,
    )
    diag = 1.0 + 2.0 / kinetic_cut
    coef = 0.5 / kinetic_cut
    padded_grad = with_halo(gradient, (("gy", 1),), SWEEPS, False)
    rows_wide = rows_y + 2 * SWEEPS
    global_rows = lax.axis_index("gy") * rows_y - SWEEPS + jnp.arange(rows_wide, dtype=jnp.int32)
    valid = ((global_rows >= 0) & (global_rows < total_y)).astype(jnp.float32)[None, :, None]
    precond = padded_grad / diag
    for sweep in range(SWEEPS):
        shifted = jnp.pad(precond, ((0, 0), (1, 1), (0, 0)))
        beside = (
            shifted[:, 2:] + shifted[:, :-2] + jnp.roll(precond, 1, 2) + jnp.roll(precond, -1, 2)
        )
        precond = (padded_grad + coef * beside) / diag * valid
    precond = precond[:, SWEEPS : SWEEPS + rows_y]
    y_global = lax.axis_index("gy") * rows_y + jnp.arange(rows_y, dtype=jnp.int32)
    z_index = jnp.arange(depth_z, dtype=jnp.int32)
    inside = (
        (y_global[None, :, None] >= regions[:, 0, None, None])
        & (y_global[None, :, None] < regions[:, 1, None, None])
        & (z_index[None, None, :] >= regions[:, 2, None, None])
        & (z_index[None, None, :] < regions[:, 3, None, None])
    )
    inside = inside.astype(jnp.float32)
    masked = (inside[:, None] * precond.reshape(block_count, block_size, rows_y, depth_z)).reshape(
        orbitals, rows_y, depth_z
    )
    new_support = support_funcs.astype(jnp.float32) - step_length * masked
    return (new_support, hamiltonian)


def solution(mesh):
    return jax.shard_map(
        local,
        mesh=mesh,
        in_specs=(
            P("gx", "gy", None),
            P("gy", None),
            P("gy", "gx", None, None),
            P("gy", "gx", None, None),
            P("gx", None),
            P("gx", None),
        ),
        out_specs=(P("gx", "gy", None), P("gy", "gx", None, None)),
        check_vma=False,
    )
```

profile of v0, /device:TPU:0, one launch (start us, length us, event | category | flops | bytes accessed | tf_op | source)
XLA Modules:
  0.0 115.5 jit_solution(4674596241081659774)
XLA Ops:
  7.2 0.0 reduce-scatter.2.cloned.1.call-start
  7.2 1.2 %copy.33 = bf16[384,4,128]{0,2,1:T(8,128)(2,1)S(1)} copy(bf16[384,4,128]{2,1,0:T(4,128)(2,1)} %param.6) | data formatting | bytes 786432 | tf_op args[0]
  8.5 0.0 copy-start.6
  8.5 0.0 copy-start.7
  8.5 0.0 copy-start.8
  8.5 1.3 %collective-permute-start = (bf16[384,1,128]{0,2,1:T(8,128)(2,1)S(1)}, bf16[384,1,128]{0,2,1:T(8,128)(2,1)S(1)}, u32[]{:S(2)}, u32[]{:S(2)}) collective-permute-start(bf16[384,1,128]{0,2,1:T(8,128)(2,1)S(1)} %get-tuple-element.28), channel_id=1, source_target_pairs={{1,0},{2,1},{3,2},{5,4},{6,5},{7,6},{9,8},{10,9},{11,10},{13,12},{... | collective-permute-start | bytes 294920 | tf_op jit(solution)/shard_map/ppermute | solution.py:21
  9.8 5.6 %collective-permute-start.1 = (bf16[384,1,128]{0,2,1:T(8,128)(2,1)S(1)}, bf16[384,1,128]{0,2,1:T(8,128)(2,1)S(1)}, u32[]{:S(2)}, u32[]{:S(2)}) collective-permute-start(bf16[384,1,128]{0,2,1:T(8,128)(2,1)S(1)} %get-tuple-element.29), channel_id=1, source_target_pairs={{0,1},{1,2},{2,3},{4,5},{5,6},{6,7},{8,9},{9,10},{10,11},{12,13},{... | collective-permute-start | bytes 294920 | tf_op jit(solution)/shard_map/ppermute | solution.py:20
  15.5 0.1 fusion.53
  15.6 0.0 copy-done.6
  15.6 0.1 iota_compare_fusion.1
  15.7 0.1 compare_and_fusion
  15.8 0.1 and_convert_fusion
  15.9 0.4 collective-permute-done
  16.3 1.3 %collective-permute-done.1 = bf16[384,1,128]{0,2,1:T(8,128)(2,1)S(1)} collective-permute-done((bf16[384,1,128]{0,2,1:T(8,128)(2,1)S(1)}, bf16[384,1,128]{0,2,1:T(8,128)(2,1)S(1)}, u32[]{:S(2)}, u32[]{:S(2)}) %collective-permute-start.1) | collective-permute-done | bytes 98336 | tf_op jit(solution)/shard_map/ppermute | solution.py:20
  17.6 0.0 copy-done.8
  17.6 0.3 fusion.33
  18.0 0.0 copy-start.4
  18.0 1.0 pad_maximum_fusion.5
  18.9 1.2 %collective-permute-start.3 = (bf16[2,384,4,128]{1,3,2,0:T(8,128)(2,1)}, bf16[2,384,4,128]{1,3,2,0:T(8,128)(2,1)}, u32[]{:S(2)}, u32[]{:S(2)}) collective-permute-start(bf16[2,384,4,128]{1,3,2,0:T(8,128)(2,1)} %pad_maximum_fusion.5), channel_id=1, source_target_pairs={{4,0},{8,4},{12,8},{16,12},{20,16},{24,20},{28,24},{0,28},{5,1},{9... | collective-permute-start | bytes 2359304 | tf_op jit(solution)/shard_map/ppermute | solution.py:21
  20.1 0.0 collective-permute-start.2
  20.1 0.1 slice.181
  20.2 0.1 copy.34
  20.3 0.1 mul.87
  20.4 1.1 copy.42
  21.5 0.0 copy-done.4
  21.5 16.1 %all_gather.7 = bf16[4,6,64,64]{3,2,1,0:T(8,128)(2,1)S(1)} all-gather(bf16[1,6,64,64]{3,2,1,0:T(8,128)(2,1)S(1)} %copy-done.4), channel_id=1, replica_groups=mesh['gx'=8,'gy'=4] {'gy'}, dimensions={0}, use_global_device_ids=true | all-gather | bytes 245760 | tf_op jit(solution)/shard_map/all_gather | solution.py:69
  37.6 1.3 %fusion.1 = bf16[6,64,18,64]{3,2,1,0:T(8,128)(2,1)S(1)} fusion(bf16[4,6,64,64]{3,2,1,0:T(8,128)(2,1)S(1)} %all_gather.7, s32[6,4]{1,0:T(8,128)S(1)} %copy.34), kind=kOutput, calls=%fused_computation.9 | convolution fusion | flops 4424112 | bytes 1081440 | tf_op jit(solution)/shard_map/akc,kaij->aicj/dot_general | solution.py:66
  38.9 0.0 copy-start.5
  38.9 2.2 %neg.11 = bf16[384,1152]{1,0:T(8,128)(2,1)} reshape(bf16[6,64,18,64]{3,2,1,0:T(8,128)(2,1)S(1)} %fusion.1) | data formatting | bytes 1769472 | tf_op jit(solution)/shard_map/neg | solution.py:73
  41.1 14.4 %all_gather.6 = bf16[4,6,64,64]{3,2,1,0:T(8,128)(2,1)S(1)} all-gather(bf16[1,6,64,64]{3,2,1,0:T(8,128)(2,1)S(1)} %copy-done.5), channel_id=1, replica_groups=mesh['gx'=8,'gy'=4] {'gy'}, dimensions={0}, use_global_device_ids=true | all-gather | bytes 245760 | tf_op jit(solution)/shard_map/all_gather | solution.py:63
  55.5 1.3 %convert_bitcast_fusion = bf16[6,64,18,64]{3,2,1,0:T(8,128)(2,1)S(1)} fusion(bf16[4,6,64,64]{3,2,1,0:T(8,128)(2,1)S(1)} %all_gather.6, s32[6,4]{1,0:T(8,128)S(1)} %copy.34), kind=kOutput, calls=%fused_computation.12 | convolution fusion | flops 3981744 | bytes 1081440 | tf_op jit(solution)/shard_map/akc,kaij->aicj/dot_general | solution.py:60
  56.8 2.2 %reshape.160 = bf16[384,1152]{1,0:T(8,128)(2,1)} reshape(bf16[6,64,18,64]{3,2,1,0:T(8,128)(2,1)S(1)} %convert_bitcast_fusion) | data formatting | bytes 1769472 | tf_op jit(solution)/shard_map/reshape | solution.py:73
  59.1 0.0 collective-permute-done.3
  59.1 0.0 collective-permute-done.2
  59.1 1.6 %pad_maximum_fusion = bf16[2,1152,4,128]{1,3,2,0:T(8,128)(2,1)S(1)} fusion(bf16[2,384,4,128]{1,3,2,0:T(8,128)(2,1)} %collective-permute-done.3, bf16[1,384,4,128]{1,3,2,0:T(8,128)(2,1)S(1)} %fusion.33, bf16[1,384,4,128]{1,3,2,0:T(8,128)(2,1)S(1)} %bitcast.43, bf16[2,384,4,128]{1,3,2,0:T(8,128)(2,1)} %collective-permute-done.2), kind=kLoop, calls=%fused_computation.10 | loop fusion | flops 9437184 | bytes 4718592 | tf_op jit(solution)/shard_map/concatenate | solution.py:22
  60.7 0.2 fusion.43
  61.0 0.2 pad_maximum_fusion.1
  61.1 1.0 copy-done.2
  62.1 0.3 copy-done.3
  62.4 1.4 %fusion.14 = f32[384,4,128]{0,2,1:T(8,128)S(1)} fusion(bf16[4,128,2304]{2,1,0:T(8,128)(2,1)S(1)} %bitcast.48, bf16[384,1152]{1,0:T(8,128)(2,1)S(1)} %copy-done.2, bf16[384,1152]{1,0:T(8,128)(2,1)S(1)} %copy-done.3), kind=kOutput, calls=%fused_computation.27 | convolution fusion | flops 909508608 | bytes 4915200 | tf_op jit(solution)/shard_map/dot_general | solution.py:77
  63.8 0.0 copy-start.1
  63.8 1.1 fusion.50
  64.9 3.9 %collective-permute-start.4 = (f32[384,3,128]{0,2,1:T(8,128)}, f32[384,3,128]{0,2,1:T(8,128)S(1)}, u32[]{:S(2)}, u32[]{:S(2)}) collective-permute-start(f32[384,3,128]{0,2,1:T(8,128)} %get-tuple-element.26), channel_id=1, source_target_pairs={{0,1},{1,2},{2,3},{4,5},{5,6},{6,7},{8,9},{9,10},{10,11},{12,13},{... | collective-permute-start | bytes 1769480 | tf_op jit(solution)/shard_map/ppermute | solution.py:20
  68.9 1.5 %collective-permute-start.5 = (f32[384,3,128]{0,2,1:T(8,128)}, f32[384,3,128]{0,2,1:T(8,128)}, u32[]{:S(2)}, u32[]{:S(2)}) collective-permute-start(f32[384,3,128]{0,2,1:T(8,128)} %get-tuple-element.27), channel_id=1, source_target_pairs={{1,0},{2,1},{3,2},{5,4},{6,5},{7,6},{9,8},{10,9},{11,10},{13,12},{... | collective-permute-start | bytes 1769480 | tf_op jit(solution)/shard_map/ppermute | solution.py:21
  70.3 0.8 fusion
  71.2 2.0 %copy.43 = f32[384,1152]{1,0:T(8,128)} copy(f32[384,1152]{0,1:T(8,128)S(1)} %fusion) | data formatting | bytes 3538944 | tf_op jit(solution)/shard_map/mul | solution.py:82
  73.1 4.5 %reshape.162 = f32[6,64,18,64]{3,2,1,0:T(8,128)} reshape(f32[384,1152]{1,0:T(8,128)} %copy.43) | data formatting | bytes 3538944 | tf_op jit(solution)/shard_map/reshape | solution.py:90
  77.7 4.2 %convolution_bitcast_fusion = f32[4,6,64,64]{3,0,2,1:T(4,128)S(1)} fusion(f32[6,64,18,64]{3,2,1,0:T(8,128)} %reshape.162, s32[6,4]{1,0:T(8,128)S(1)} %copy.34), kind=kOutput, calls=%fused_computation.30 | convolution fusion | flops 21234096 | bytes 2162784 | tf_op jit(solution)/shard_map/akc,aicj->kaij/dot_general | solution.py:93
  81.8 1.0 copy.44
  82.8 0.0 reduce-scatter.2.cloned.1.call-update
  82.8 0.0 collective-permute-done.4
  82.9 0.0 collective-permute-done.5
  82.9 1.2 %broadcast_multiply_fusion = f32[384,10,128]{0,2,1:T(8,128)S(1)} fusion(f32[384,3,128]{0,2,1:T(8,128)} %collective-permute-done.5, f32[384,4,128]{0,2,1:T(8,128)S(1)} %fusion.14, f32[384,3,128]{0,2,1:T(8,128)S(1)} %collective-permute-done.4), kind=kLoop, calls=%fused_computation.31 | loop fusion | flops 1474560 | bytes 3932160 | tf_op jit(solution)/shard_map/div | solution.py:104
  84.1 0.4 fusion.48
  84.5 1.8 %fusion.7 = f32[384,10,128]{0,2,1:T(8,128)S(1)} fusion(f32[384,10,128]{0,2,1:T(8,128)S(1)} %broadcast_multiply_fusion, f32[384,10,127]{0,2,1:T(8,128)S(1)} %get-tuple-element.23, f32[384,10,1]{0,2,1:T(1,128)S(1)} %get-tuple-element.25, f32[384,10,1]{0,2,1:T(1,128)S(1)} %get-tuple-element.24, f32[384,10,127]{0,2,1:T(8,128)S(1)} %get-tuple-element.22, ...), kind=kLoop, calls=%fused_computation.18 | loop fusion | flops 4915200 | bytes 9830440 | tf_op jit(solution)/shard_map/mul | solution.py:110
  86.4 0.3 fusion.46
  86.7 1.8 %fusion.13 = (f32[384,10,128]{0,2,1:T(8,128)S(1)}, f32[384,10,128]{0,2,1:T(8,128)S(1)}) fusion(f32[384,10,128]{0,2,1:T(8,128)S(1)} %fusion.7, f32[384,10,127]{0,2,1:T(8,128)S(1)} %get-tuple-element.19, f32[384,10,1]{0,2,1:T(1,128)S(1)} %get-tuple-element.21, f32[384,10,1]{0,2,1:T(1,128)S(1)} %get-tuple-element.20, f32[384,10,127]{0,2,1:T(8,128)S(1)} %get-tuple-element.18, ...), kind=kLoop, calls=%fused_computation.24 | loop fusion | flops 4915200 | bytes 11796520 | tf_op jit(solution)/shard_map/mul | solution.py:110
  88.5 0.5 pad_slice_fusion.1
  89.0 0.0 copy-start
  89.0 0.3 fusion.45
  89.4 0.8 copy-done
  90.1 0.5 fusion.20
  90.6 1.1 copy.45
  91.7 17.0 %reduce-scatter.2.cloned.1.call-done = f32[1,6,64,64]{3,2,1,0:T(8,128)} async-done(((f32[4,6,64,64]{3,2,1,0:T(8,128)}), f32[1,6,64,64]{3,2,1,0:T(8,128)}) %reduce-scatter.2.cloned.1.call-update) | async-done | bytes 98320 | tf_op jit(solution)/shard_map/reduce_scatter | solution.py:92
  (14 shorter events, 0.2 us)
Async XLA Ops:
  7.2 101.5 %reduce-scatter.2.cloned.1.call-start = ((), (), s32[]{:S(2)}) async-start(), calls=%async_computation.1 | async-start | bytes 983040 | tf_op jit(solution)/shard_map/reduce_scatter | solution.py:92
  8.5 7.1 %copy-start.6 = (s32[6,4]{0,1:T(4,128)S(1)}, s32[6,4]{0,1:T(4,128)}, u32[]{:S(2)}) copy-start(s32[6,4]{0,1:T(4,128)} %param.11) | copy-start | bytes 292
  8.5 7.4 %copy-start.7 = (s32[6,4]{0,1:T(4,128)S(1)}, s32[6,4]{0,1:T(4,128)}, u32[]{:S(2)}) copy-start(s32[6,4]{0,1:T(4,128)} %param.10) | copy-start | bytes 292
  8.5 9.1 %copy-start.8 = (f32[4,128]{1,0:T(4,128)S(1)}, f32[4,128]{1,0:T(4,128)}, u32[]{:S(2)}) copy-start(f32[4,128]{1,0:T(4,128)} %param.7) | copy-start | bytes 6148
  8.5 7.7 %collective-permute-start = (bf16[384,1,128]{0,2,1:T(8,128)(2,1)S(1)}, bf16[384,1,128]{0,2,1:T(8,128)(2,1)S(1)}, u32[]{:S(2)}, u32[]{:S(2)}) collective-permute-start(bf16[384,1,128]{0,2,1:T(8,128)(2,1)S(1)} %get-tuple-element.28), channel_id=1, source_target_pairs={{1,0},{2,1},{3,2},{5,4},{6,5},{7,6},{9,8},{10,9},{11,10},{13,12},{... | collective-permute-start | bytes 294920 | tf_op jit(solution)/shard_map/ppermute | solution.py:21
  9.8 7.8 %collective-permute-start.1 = (bf16[384,1,128]{0,2,1:T(8,128)(2,1)S(1)}, bf16[384,1,128]{0,2,1:T(8,128)(2,1)S(1)}, u32[]{:S(2)}, u32[]{:S(2)}) collective-permute-start(bf16[384,1,128]{0,2,1:T(8,128)(2,1)S(1)} %get-tuple-element.29), channel_id=1, source_target_pairs={{0,1},{1,2},{2,3},{4,5},{5,6},{6,7},{8,9},{9,10},{10,11},{12,13},{... | collective-permute-start | bytes 294920 | tf_op jit(solution)/shard_map/ppermute | solution.py:20
  18.0 3.6 %copy-start.4 = (bf16[1,6,64,64]{3,2,1,0:T(8,128)(2,1)S(1)}, bf16[1,6,64,64]{3,2,1,0:T(8,128)(2,1)}, u32[]{:S(2)}) copy-start(bf16[1,6,64,64]{3,2,1,0:T(8,128)(2,1)} %param.9) | copy-start | bytes 147460
  18.9 40.1 %collective-permute-start.3 = (bf16[2,384,4,128]{1,3,2,0:T(8,128)(2,1)}, bf16[2,384,4,128]{1,3,2,0:T(8,128)(2,1)}, u32[]{:S(2)}, u32[]{:S(2)}) collective-permute-start(bf16[2,384,4,128]{1,3,2,0:T(8,128)(2,1)} %pad_maximum_fusion.5), channel_id=1, source_target_pairs={{4,0},{8,4},{12,8},{16,12},{20,16},{24,20},{28,24},{0,28},{5,1},{9... | collective-permute-start | bytes 2359304 | tf_op jit(solution)/shard_map/ppermute | solution.py:21
  20.1 38.9 %collective-permute-start.2 = (bf16[2,384,4,128]{1,3,2,0:T(8,128)(2,1)}, bf16[2,384,4,128]{1,3,2,0:T(8,128)(2,1)}, u32[]{:S(2)}, u32[]{:S(2)}) collective-permute-start(bf16[2,384,4,128]{1,3,2,0:T(8,128)(2,1)} %pad_maximum_fusion.5), channel_id=1, source_target_pairs={{0,4},{4,8},{8,12},{12,16},{16,20},{20,24},{24,28},{28,0},{1,5},{5... | collective-permute-start | bytes 2359304 | tf_op jit(solution)/shard_map/ppermute | solution.py:20
  38.9 2.2 %copy-start.5 = (bf16[1,6,64,64]{3,2,1,0:T(8,128)(2,1)S(1)}, bf16[1,6,64,64]{3,2,1,0:T(8,128)(2,1)}, u32[]{:S(2)}) copy-start(bf16[1,6,64,64]{3,2,1,0:T(8,128)(2,1)} %param.8) | copy-start | bytes 147460
  60.9 1.2 %copy-start.2 = (bf16[384,1152]{1,0:T(8,128)(2,1)S(1)}, bf16[384,1152]{1,0:T(8,128)(2,1)}, u32[]{:S(2)}) copy-start(bf16[384,1152]{1,0:T(8,128)(2,1)} %neg.11) | copy-start | bytes 2654212
  60.9 1.4 %copy-start.3 = (bf16[384,1152]{1,0:T(8,128)(2,1)S(1)}, bf16[384,1152]{1,0:T(8,128)(2,1)}, u32[]{:S(2)}) copy-start(bf16[384,1152]{1,0:T(8,128)(2,1)} %reshape.160) | copy-start | bytes 2654212
  63.8 6.6 %copy-start.1 = (bf16[384,4,128]{2,1,0:T(4,128)(2,1)S(1)}, bf16[384,4,128]{2,1,0:T(4,128)(2,1)}, u32[]{:S(2)}) copy-start(bf16[384,4,128]{2,1,0:T(4,128)(2,1)} %param.6) | copy-start | bytes 1179652
  64.9 17.9 %collective-permute-start.4 = (f32[384,3,128]{0,2,1:T(8,128)}, f32[384,3,128]{0,2,1:T(8,128)S(1)}, u32[]{:S(2)}, u32[]{:S(2)}) collective-permute-start(f32[384,3,128]{0,2,1:T(8,128)} %get-tuple-element.26), channel_id=1, source_target_pairs={{0,1},{1,2},{2,3},{4,5},{5,6},{6,7},{8,9},{9,10},{10,11},{12,13},{... | collective-permute-start | bytes 1769480 | tf_op jit(solution)/shard_map/ppermute | solution.py:20
  68.9 14.0 %collective-permute-start.5 = (f32[384,3,128]{0,2,1:T(8,128)}, f32[384,3,128]{0,2,1:T(8,128)}, u32[]{:S(2)}, u32[]{:S(2)}) collective-permute-start(f32[384,3,128]{0,2,1:T(8,128)} %get-tuple-element.27), channel_id=1, source_target_pairs={{1,0},{2,1},{3,2},{5,4},{6,5},{7,6},{9,8},{10,9},{11,10},{13,12},{... | collective-permute-start | bytes 1769480 | tf_op jit(solution)/shard_map/ppermute | solution.py:21
  89.0 1.1 copy-start
Sparse Core Ops, SparseCore 0:
  83.0 25.6 reduce-scatter.1
where the time goes:
time: 116 us
  blocking collectives  30.5 us (26%)
  local copies, waits for them, and re-layouts  20.8 us (18%)
  waiting for transfers between devices  18.7 us (16%)
  between operations  14.4 us (12%)
  starting transfers between devices  13.5 us (12%)
  matrix products  8.97 us (8%)
  other arithmetic  8.67 us (7%)
    reduce_scatter x1, waiting for transfers between devices, local(): lax.psum_scatter(jnp.einsum('akc,aicj->kaij', picks, blocked, precision=l...  17 us
    all_gather x1, blocking collectives, local(): lax.all_gather(weighted, 'gy', axis=0, tiled=True)  16.1 us
    all_gather x1, blocking collectives, local(): lax.all_gather(kernel, 'gy', axis=0, tiled=True)  14.4 us
    ppermute x3, starting transfers between devices, with_halo(): before = lax.ppermute(last, axis, up)  9.53 us
    reshape x1, local copies, waits for them, and re-layouts, local(): intersections.reshape(block_count, block_size, slot_count, block_size)  4.53 us
    unnamed x20, local copies, waits for them, and re-layouts  4.46 us
    dot_general x1, matrix products, local(): jnp.einsum('akc,aicj->kaij', picks, blocked, precision=lax.Precision.HIGH...  4.17 us
    ppermute x3, starting transfers between devices, with_halo(): after = lax.ppermute(leading, axis, down)  3.95 us
  transfers between devices with their start and end apart: 7, of which 3 were waited for; matrix products, arithmetic and copies ran while one was open for 25% of the time, Pallas kernels for 0%

commit v1 on v0

v1 whole, which is shorter than its diff:
```python
import functools

import jax
import jax.numpy as jnp
from jax import lax
from jax.experimental import pallas as pl
from jax.experimental.pallas import tpu as pltpu
from jax.sharding import PartitionSpec as P

SWEEPS = 3
CHUNK = 2
kinetic_cut = 1.0
step_length = 0.5
f32 = jnp.float32
bf16 = jnp.bfloat16


def remote(src, dst, send, recv, **device):
    return pltpu.make_async_remote_copy(
        src_ref=src,
        dst_ref=dst,
        send_sem=send,
        recv_sem=recv,
        device_id=device,
        device_id_type=pl.DeviceIdType.MESH,
    )


def loop(count, body):
    def step(i, carry):
        body(i)
        return carry

    lax.fori_loop(0, count, step, 0)


def kernel_body(
    n_gx, n_gy, rows_y,
    cols_ref, regs_ref, pot_ref, x_ref, kern_ref, wght_ref,
    out_ref, ham_ref,
    raw, wide, near_phi, near_app, edge_send, edge_recv, pack, packs,
    grad, halo_send, halo_recv, part, part_recv,
    x_send, x_recv, e_send, e_recv, k_send, k_recv, k_own, g_send, g_recv, h_send, h_recv,
):
    gx, gy = lax.axis_index("gx"), lax.axis_index("gy")
    right, left = lax.rem(gx + 1, n_gx), lax.rem(gx + n_gx - 1, n_gx)
    own_slots, nb, size = kern_ref.shape[:3]
    slots = own_slots * n_gy
    depth = x_ref.shape[1]
    brick = size * rows_y
    chunks = nb // CHUNK
    rows = CHUNK * brick
    half = size // 2
    has_low, has_high = gy > 0, gy < n_gy - 1
    volume = 1.0 / (rows_y * n_gy * depth)

    barrier = pltpu.get_barrier_semaphore()
    for device in (left, right):
        pl.semaphore_signal(barrier, device_id={"gx": device}, device_id_type=pl.DeviceIdType.MESH)
    for off in range(1, n_gy):
        pl.semaphore_signal(
            barrier, device_id={"gy": lax.rem(gy + off, n_gy)}, device_id_type=pl.DeviceIdType.MESH
        )
    for j in range(own_slots):
        for a in range(nb):
            pack[j, a] = jnp.concatenate([kern_ref[j, a], wght_ref[j, a]], axis=1)
    pl.semaphore_wait(barrier, 2 + n_gy - 1)

    def x_copy(to_right, c):
        piece = pl.ds(pl.multiple_of(c * rows, rows), rows)
        group = 0 if to_right else 2
        return remote(
            x_ref.at[piece], raw.at[group, piece], x_send.at[group, c], x_recv.at[group, c],
            gx=right if to_right else left,
        )

    def start_x(c):
        x_copy(True, c).start()
        x_copy(False, c).start()

    loop(chunks, start_x)

    def k_copy(off):
        mine = pl.ds(gy * own_slots, own_slots)
        return remote(
            pack, packs.at[mine], k_send.at[off - 1], k_recv.at[off - 1], gy=lax.rem(gy + off, n_gy)
        )

    for off in range(1, n_gy):
        k_copy(off).start()
    own_copy = pltpu.make_async_copy(pack, packs.at[pl.ds(gy * own_slots, own_slots)], k_own)
    own_copy.start()

    def base_of(p):
        return pl.multiple_of(p * brick, brick)

    def spread(group, c, source):
        for i in range(CHUNK):
            b = c * CHUNK + i
            p = group * nb + b
            wide[pl.ds(base_of(p), brick), :] = source(b).astype(f32)
            for y in range(rows_y):
                row = wide[pl.ds(base_of(p) + y, size, stride=rows_y), :].astype(bf16)
                near_phi[p, :, y * depth : (y + 1) * depth] = row
                if y == 0:
                    edge_send[0, p] = row
                if y == rows_y - 1:
                    edge_send[1, p] = row

    def edge_copy(side, group, c):
        piece = pl.ds(group * nb + c * CHUNK, CHUNK)
        index = group * chunks + c
        return remote(
            edge_send.at[side, piece], edge_recv.at[1 - side, piece],
            e_send.at[side, index], e_recv.at[1 - side, index],
            gy=jnp.maximum(gy - 1, 0) if side == 0 else jnp.minimum(gy + 1, n_gy - 1),
        )

    def both_sides(action):
        pl.when(has_low)(lambda: action(0))
        pl.when(has_high)(lambda: action(1))

    def own_chunk(c):
        spread(1, c, lambda b: x_ref[pl.ds(pl.multiple_of(b * brick, brick), brick), :])
        both_sides(lambda side: edge_copy(side, 1, c).start())

    def far_chunk(group, c):
        piece = pl.ds(pl.multiple_of(c * rows, rows), rows)
        remote(
            x_ref.at[piece], raw.at[group, piece], x_send.at[group, c], x_recv.at[group, c], gx=right
        ).wait_recv()
        spread(group, c, lambda b: raw[group, pl.ds(pl.multiple_of(b * brick, brick), brick), :])
        both_sides(lambda side: edge_copy(side, group, c).start())

    def apply_chunk(group, c):
        pl.when(has_low)(lambda: edge_copy(1, group, c).wait_recv())
        pl.when(has_high)(lambda: edge_copy(0, group, c).wait_recv())
        for i in range(CHUNK):
            p = group * nb + c * CHUNK + i
            base = base_of(p)
            line = [edge_recv[0, p].astype(f32)]
            line += [wide[pl.ds(base + y, size, stride=rows_y), :] for y in range(rows_y)]
            line += [edge_recv[1, p].astype(f32)]
            for y in range(rows_y):
                center = line[y + 1]
                beside = (
                    line[y + 2] + line[y] + pltpu.roll(center, 1, 1) + pltpu.roll(center, depth - 1, 1)
                )
                applied = -0.5 * (beside - 4.0 * center) + pot_ref[y : y + 1, :] * center
                near_app[p, :, y * depth : (y + 1) * depth] = applied.astype(bf16)

    @pl.when(gy == 0)
    def _():
        edge_recv[0] = jnp.zeros(edge_recv.shape[1:], bf16)
        halo_recv[0] = jnp.zeros(halo_recv.shape[1:], bf16)

    @pl.when(gy == n_gy - 1)
    def _():
        edge_recv[1] = jnp.zeros(edge_recv.shape[1:], bf16)
        halo_recv[1] = jnp.zeros(halo_recv.shape[1:], bf16)

    first = 2 - 2 * lax.rem(gx, 2)
    second = 2 - first
    loop(chunks, own_chunk)
    loop(chunks, lambda c: far_chunk(first, c))
    loop(chunks, lambda c: apply_chunk(1, c))
    for off in range(1, n_gy):
        k_copy(off).wait_recv()
    own_copy.wait()
    loop(chunks, lambda c: far_chunk(second, c))
    loop(chunks, lambda c: apply_chunk(first, c))
    loop(chunks, lambda c: apply_chunk(second, c))

    def picks(a):
        start = nb * n_gx + nb - nb * gx
        found = [lax.rem(cols_ref[a, k] + start, nb * n_gx) for k in range(slots)]
        return [jnp.minimum(p, 3 * nb - 1) for p in found]

    def halo_copy(side, a):
        return remote(
            halo_send.at[side, a], halo_recv.at[1 - side, a], g_send.at[side, a], g_recv.at[1 - side, a],
            gy=jnp.maximum(gy - 1, 0) if side == 0 else jnp.minimum(gy + 1, n_gy - 1),
        )

    def gradient_of(a):
        where = picks(a)
        blocks = [packs[k, a] for k in range(slots)]
        mixing = jnp.concatenate(
            [b[:, :size] for b in blocks] + [-b[:, size:] for b in blocks], axis=1
        )
        source = jnp.concatenate([near_app[p] for p in where] + [near_phi[p] for p in where], axis=0)
        total = jnp.dot(mixing, source, preferred_element_type=f32)
        for y in range(rows_y):
            piece = total[:, y * depth : (y + 1) * depth]
            grad[a, y] = piece
            if y < SWEEPS:
                halo_send[0, a, y] = piece.astype(bf16)
            if y >= rows_y - SWEEPS:
                halo_send[1, a, y - rows_y + SWEEPS] = piece.astype(bf16)
        both_sides(lambda side: halo_copy(side, a).start())

    loop(nb, gradient_of)

    def part_of(a):
        source = jnp.concatenate([near_app[p] for p in picks(a)], axis=0)
        block = lax.dot_general(
            near_phi[nb + a], source, (((1,), (1,)), ((), ())), preferred_element_type=f32
        ) * volume
        for k in range(slots):
            one = block[:, k * size : (k + 1) * size]
            part[k, a] = jnp.concatenate([one[:half], one[half:]], axis=1)

    loop(nb, part_of)

    def part_copy(off):
        peer = lax.rem(gy + off, n_gy)
        return remote(
            part.at[pl.ds(peer * own_slots, own_slots)], part_recv.at[off - 1],
            h_send.at[off - 1], h_recv.at[off - 1], gy=peer,
        )

    for off in range(1, n_gy):
        part_copy(off).start()

    diag = 1.0 + 2.0 / kinetic_cut
    coef = 0.5 / kinetic_cut
    low, high = jnp.where(has_low, 1.0, 0.0).astype(f32), jnp.where(has_high, 1.0, 0.0).astype(f32)
    z_index = lax.broadcasted_iota(jnp.int32, (size, depth), 1)

    def finish(a):
        pl.when(has_low)(lambda: halo_copy(1, a).wait_recv())
        pl.when(has_high)(lambda: halo_copy(0, a).wait_recv())
        field = [halo_recv[0, a, i].astype(f32) for i in range(SWEEPS)]
        field += [grad[a, y] for y in range(rows_y)]
        field += [halo_recv[1, a, i].astype(f32) for i in range(SWEEPS)]
        field = [value * (1.0 / diag) for value in field]
        now = list(field)
        for sweep in range(1, SWEEPS + 1):
            later = list(now)
            for i in range(sweep, rows_y + 2 * SWEEPS - sweep):
                beside = now[i - 1] + now[i + 1]
                beside = beside + pltpu.roll(now[i], 1, 1) + pltpu.roll(now[i], depth - 1, 1)
                value = field[i] + (coef / diag) * beside
                if i < SWEEPS:
                    value = value * low
                if i >= rows_y + SWEEPS:
                    value = value * high
                later[i] = value
            now = later
        z_in = (z_index >= regs_ref[a, 2]) & (z_index < regs_ref[a, 3])
        base = base_of(nb + a)
        for y in range(rows_y):
            spot = gy * rows_y + y
            y_in = jnp.where((spot >= regs_ref[a, 0]) & (spot < regs_ref[a, 1]), step_length, 0.0)
            masked = jnp.where(z_in, now[SWEEPS + y] * y_in.astype(f32), 0.0)
            phi = wide[pl.ds(base + y, size, stride=rows_y), :]
            out_ref[pl.ds(pl.multiple_of(a * brick, brick) + y, size, stride=rows_y), :] = phi - masked

    loop(nb, finish)

    for off in range(1, n_gy):
        part_copy(off).wait_recv()
    for j in range(own_slots):
        for a in range(nb):
            total = part[gy * own_slots + j, a]
            for off in range(1, n_gy):
                total = total + part_recv[off - 1, j, a]
            ham_ref[j, a, :half, :] = total[:, :size]
            ham_ref[j, a, half:, :] = total[:, size:]

    def sent_x(c):
        x_copy(True, c).wait_send()
        x_copy(False, c).wait_send()

    loop(chunks, sent_x)
    for group in range(3):
        loop(chunks, lambda c: both_sides(lambda side: edge_copy(side, group, c).wait_send()))
    loop(nb, lambda a: both_sides(lambda side: halo_copy(side, a).wait_send()))
    for off in range(1, n_gy):
        k_copy(off).wait_send()
        part_copy(off).wait_send()


def local(n_gx, n_gy, support_funcs, potential, kernel, weighted, columns, regions):
    own_slots, nb, size = kernel.shape[:3]
    orbitals, rows_y, depth = support_funcs.shape
    slots = own_slots * n_gy
    flat = orbitals * rows_y
    chunks = nb // CHUNK
    vmem = pl.BlockSpec(memory_space=pltpu.VMEM)
    smem = pl.BlockSpec(memory_space=pltpu.SMEM)
    dma = pltpu.SemaphoreType.DMA
    new_support, hamiltonian = pl.pallas_call(
        functools.partial(kernel_body, n_gx, n_gy, rows_y),
        out_shape=(
            jax.ShapeDtypeStruct((flat, depth), f32),
            jax.ShapeDtypeStruct((own_slots, nb, size, size), f32),
        ),
        in_specs=[smem, smem, vmem, vmem, vmem, vmem],
        out_specs=(vmem, vmem),
        scratch_shapes=[
            pltpu.VMEM((3, flat, depth), bf16),
            pltpu.VMEM((3 * flat, depth), f32),
            pltpu.VMEM((3 * nb, size, rows_y * depth), bf16),
            pltpu.VMEM((3 * nb, size, rows_y * depth), bf16),
            pltpu.VMEM((2, 3 * nb, size, depth), bf16),
            pltpu.VMEM((2, 3 * nb, size, depth), bf16),
            pltpu.VMEM((own_slots, nb, size, 2 * size), bf16),
            pltpu.VMEM((slots, nb, size, 2 * size), bf16),
            pltpu.VMEM((nb, rows_y, size, depth), f32),
            pltpu.VMEM((2, nb, SWEEPS, size, depth), bf16),
            pltpu.VMEM((2, nb, SWEEPS, size, depth), bf16),
            pltpu.VMEM((slots, nb, size // 2, 2 * size), f32),
            pltpu.VMEM((n_gy - 1, own_slots, nb, size // 2, 2 * size), f32),
            dma((3, chunks)),
            dma((3, chunks)),
            dma((2, 3 * chunks)),
            dma((2, 3 * chunks)),
            dma((n_gy - 1,)),
            dma((n_gy - 1,)),
            dma(()),
            dma((2, nb)),
            dma((2, nb)),
            dma((n_gy - 1,)),
            dma((n_gy - 1,)),
        ],
        compiler_params=pltpu.CompilerParams(
            collective_id=0, has_side_effects=True, vmem_limit_bytes=40 * 1024 * 1024
        ),
    )(columns, regions, potential, support_funcs.reshape(flat, depth), kernel, weighted)
    return (new_support.reshape(orbitals, rows_y, depth), hamiltonian)


def solution(mesh):
    return jax.shard_map(
        functools.partial(local, mesh.shape["gx"], mesh.shape["gy"]),
        mesh=mesh,
        in_specs=(
            P("gx", "gy", None),
            P("gy", None),
            P("gy", "gx", None, None),
            P("gy", "gx", None, None),
            P("gx", None),
            P("gx", None),
        ),
        out_specs=(P("gx", "gy", None), P("gy", "gx", None, None)),
        check_vma=False,
    )
```

time: 116 us -> 44.7 us (0.39)
  Pallas kernels: 0 us -> 38 us
  blocking collectives: 30.5 us -> 0 us
  waiting for transfers between devices: 18.7 us -> 0 us
  local copies, waits for them, and re-layouts: 20.8 us -> 5.8 us
  between operations: 14.4 us -> 0.65 us
  starting transfers between devices: 13.5 us -> 0 us
  matrix products: 8.97 us -> 0 us
  other arithmetic: 8.67 us -> 0 us
    pallas_call x0 -> x1, Pallas kernels: none -> 38 us  [local(): pl.pallas_call(functools.partial(kernel_body, n_gx, n_gy, rows_y), out_sh...]
    all_gather x2 -> x0, blocking collectives: 30.5 us -> none  [the longest x1 16.1 us: local(): lax.all_gather(weighted, 'gy', axis=0, tiled=True)]
    reduce_scatter x1 -> x0, waiting for transfers between devices: 17 us -> none  [local(): lax.psum_scatter(jnp.einsum('akc,aicj->kaij', picks, blocked, precision=l...]
    ppermute x6 -> x0, starting transfers between devices: 13.5 us -> none  [the longest x3 9.53 us: with_halo(): before = lax.ppermute(last, axis, up)]
    dot_general x5 -> x0, matrix products: 8.97 us -> none  [the longest x1 4.17 us: local(): jnp.einsum('akc,aicj->kaij', picks, blocked, precision=lax.Precision.HIGH...]
    reshape x2 -> x0, local copies, waits for them, and re-layouts: 6.77 us -> none  [the longest x1 4.53 us: local(): intersections.reshape(block_count, block_size, slot_count, block_size)]
    mul x3 -> x0, other arithmetic: 3.6 us -> none  [local(): precond = (padded_grad + coef * beside) / diag * valid]
    mul x3 -> x0, local copies, waits for them, and re-layouts: 3.15 us -> none  [the longest x1 1.95 us: local(): lax.dot_general(support_funcs.reshape(orbitals, cells), applied_near.resh...]
  transfers between devices with their start and end apart: 7 -> 0, of which waited for: 3 -> 0; matrix products, arithmetic and copies ran while one was open for 25% -> 0% of each run, Pallas kernels for 0% -> 0%
where the time goes in v1:
time: 44.7 us; the launch traced here: 44.5 us
  Pallas kernels  38 us (85%)
  local copies, waits for them, and re-layouts  5.8 us (13%)
  between operations  0.65 us (1%)
    pallas_call x1, Pallas kernels, local(): pl.pallas_call(functools.partial(kernel_body, n_gx, n_gy, rows_y), out_sh...  38 us
    unnamed x14, local copies, waits for them, and re-layouts  5.8 us

profile of v1, /device:TPU:0, one launch (start us, length us, event | category | flops | bytes accessed | tf_op | source)
XLA Modules:
  0.0 44.5 jit_solution(12684322875437565568)
XLA Ops:
  0.6 0.0 copy-start.4
  0.6 0.8 %copy.8.cols_ref = s32[6,4]{1,0:T(8,128)S(1)} copy(s32[6,4]{0,1:T(4,128)} %param.10) | data formatting | bytes 192 | tf_op args[4]
  1.4 0.0 copy-done.4
  1.4 0.0 copy-start.3
  1.4 0.1 copy.9.regs_ref
  1.5 0.6 %copy-done.3 = f32[4,128]{1,0:T(4,128)S(1)} copy-done((f32[4,128]{1,0:T(4,128)S(1)}, f32[4,128]{1,0:T(4,128)}, u32[]{:S(2)}) %copy-start.3) | copy-done | bytes 2072
  2.1 0.0 copy-start
  2.1 1.0 %copy-done = bf16[384,4,128]{2,1,0:T(4,128)(2,1)S(1)} copy-done((bf16[384,4,128]{2,1,0:T(4,128)(2,1)S(1)}, bf16[384,4,128]{2,1,0:T(4,128)(2,1)}, u32[]{:S(2)}) %copy-start) | copy-done | bytes 393240
  3.1 0.0 copy-start.1
  3.1 0.9 %copy-done.1 = bf16[1,6,64,64]{3,2,1,0:T(8,128)(2,1)S(1)} copy-done((bf16[1,6,64,64]{3,2,1,0:T(8,128)(2,1)S(1)}, bf16[1,6,64,64]{3,2,1,0:T(8,128)(2,1)}, u32[]{:S(2)}) %copy-start.1) | copy-done | bytes 49176
  4.0 0.0 copy-start.2
  4.0 0.9 %copy-done.2 = bf16[1,6,64,64]{3,2,1,0:T(8,128)(2,1)S(1)} copy-done((bf16[1,6,64,64]{3,2,1,0:T(8,128)(2,1)S(1)}, bf16[1,6,64,64]{3,2,1,0:T(8,128)(2,1)}, u32[]{:S(2)}) %copy-start.2) | copy-done | bytes 49176
  4.9 38.0 %shard_map.77 = (f32[1536,128]{1,0:T(8,128)S(1)}, f32[1,6,64,64]{3,2,1,0:T(8,128)S(1)}) custom-call(s32[6,4]{1,0:T(8,128)S(1)} %copy.8.cols_ref, s32[6,4]{1,0:T(8,128)S(1)} %copy.9.regs_ref, f32[4,128]{1,0:T(4,128)S(1)} %copy-done.3, bf16[1536,128]{1,0:T(8,128)(2,1)S(1)} %bitcast.3, bf16[1,6,64,64]{3,2,1,0:T(8,128)(2,1)S(1)} %copy-done.1, ...), custom_call_target="tpu_custom_call" | custom-call | tf_op jit(solution)/shard_map/pallas_call | solution.py:293
  42.9 0.9 %copy.12 = f32[384,4,128]{2,1,0:T(4,128)} copy(f32[384,4,128]{2,1,0:T(4,128)S(1)} %bitcast.2) | data formatting | bytes 1572864
  43.8 0.7 %copy.13 = f32[1,6,64,64]{3,2,1,0:T(8,128)} copy(f32[1,6,64,64]{3,2,1,0:T(8,128)S(1)} %get-tuple-element.9) | data formatting | bytes 196608
Async XLA Ops:
  0.6 0.8 %copy-start.4 = (s32[6,4]{0,1:T(4,128)S(1)}, s32[6,4]{0,1:T(4,128)}, u32[]{:S(2)}) copy-start(s32[6,4]{0,1:T(4,128)} %param.11) | copy-start | bytes 292
  1.4 0.7 %copy-start.3 = (f32[4,128]{1,0:T(4,128)S(1)}, f32[4,128]{1,0:T(4,128)}, u32[]{:S(2)}) copy-start(f32[4,128]{1,0:T(4,128)} %pot_ref.1) | copy-start | bytes 6148
  2.1 1.0 %copy-start = (bf16[384,4,128]{2,1,0:T(4,128)(2,1)S(1)}, bf16[384,4,128]{2,1,0:T(4,128)(2,1)}, u32[]{:S(2)}) copy-start(bf16[384,4,128]{2,1,0:T(4,128)(2,1)} %param.6) | copy-start | bytes 1179652
  3.1 0.9 %copy-start.1 = (bf16[1,6,64,64]{3,2,1,0:T(8,128)(2,1)S(1)}, bf16[1,6,64,64]{3,2,1,0:T(8,128)(2,1)}, u32[]{:S(2)}) copy-start(bf16[1,6,64,64]{3,2,1,0:T(8,128)(2,1)} %kern_ref.1) | copy-start | bytes 147460
  4.0 0.9 %copy-start.2 = (bf16[1,6,64,64]{3,2,1,0:T(8,128)(2,1)S(1)}, bf16[1,6,64,64]{3,2,1,0:T(8,128)(2,1)}, u32[]{:S(2)}) copy-start(bf16[1,6,64,64]{3,2,1,0:T(8,128)(2,1)} %wght_ref.1) | copy-start | bytes 147460

commit v2 on v1

--- a/solution.py
+++ b/solution.py
@@ -26,6 +26,11 @@
     )
 
 
+def unrolled(count, body):
+    for i in range(count):
+        body(i)
+
+
 def loop(count, body):
     def step(i, carry):
         body(i)
@@ -36,11 +41,11 @@
 
 def kernel_body(
     n_gx, n_gy, rows_y,
-    cols_ref, regs_ref, pot_ref, x_ref, kern_ref, wght_ref,
+    cols_hbm, regs_hbm, pot_hbm, x_hbm, kern_hbm, wght_hbm,
     out_ref, ham_ref,
-    raw, wide, near_phi, near_app, edge_send, edge_recv, pack, packs,
-    grad, halo_send, halo_recv, part, part_recv,
-    x_send, x_recv, e_send, e_recv, k_send, k_recv, k_own, g_send, g_recv, h_send, h_recv,
+    cols_ref, regs_ref, pot_ref, x_ref, kern_ref, wght_ref, raw, wide, near_phi, near_app, edge_send, edge_recv, pack, packs,
+    grad, halo_send, halo_recv, part, part_half, part_recv, half_recv, in_sem,
+    x_send, x_recv, e_send, e_recv, k_send, k_recv, k_own, g_send, g_recv, h_send, h_recv, b_send, b_recv,
 ):
     gx, gy = lax.axis_index("gx"), lax.axis_index("gy")
     right, left = lax.rem(gx + 1, n_gx), lax.rem(gx + n_gx - 1, n_gx)
@@ -54,6 +59,13 @@
     has_low, has_high = gy > 0, gy < n_gy - 1
     volume = 1.0 / (rows_y * n_gy * depth)
 
+    pairs = (
+        (x_hbm, x_ref), (kern_hbm, kern_ref), (wght_hbm, wght_ref),
+        (pot_hbm, pot_ref), (cols_hbm, cols_ref), (regs_hbm, regs_ref),
+    )
+    loads = [pltpu.make_async_copy(src, dst, in_sem.at[i]) for i, (src, dst) in enumerate(pairs)]
+    for load in loads:
+        load.start()
     barrier = pltpu.get_barrier_semaphore()
     for device in (left, right):
         pl.semaphore_signal(barrier, device_id={"gx": device}, device_id_type=pl.DeviceIdType.MESH)
@@ -61,6 +73,8 @@
         pl.semaphore_signal(
             barrier, device_id={"gy": lax.rem(gy + off, n_gy)}, device_id_type=pl.DeviceIdType.MESH
         )
+    loads[1].wait()
+    loads[2].wait()
     for j in range(own_slots):
         for a in range(nb):
             pack[j, a] = jnp.concatenate([kern_ref[j, a], wght_ref[j, a]], axis=1)
@@ -70,7 +84,7 @@
         piece = pl.ds(pl.multiple_of(c * rows, rows), rows)
         group = 0 if to_right else 2
         return remote(
-            x_ref.at[piece], raw.at[group, piece], x_send.at[group, c], x_recv.at[group, c],
+            x_hbm.at[piece], raw.at[group, piece], x_send.at[group, c], x_recv.at[group, c],
             gx=right if to_right else left,
         )
 
@@ -92,6 +106,8 @@
     own_copy.start()
 
     def base_of(p):
+        if isinstance(p, int):
+            return p * brick
         return pl.multiple_of(p * brick, brick)
 
     def spread(group, c, source):
@@ -127,7 +143,7 @@
     def far_chunk(group, c):
         piece = pl.ds(pl.multiple_of(c * rows, rows), rows)
         remote(
-            x_ref.at[piece], raw.at[group, piece], x_send.at[group, c], x_recv.at[group, c], gx=right
+            x_hbm.at[piece], raw.at[group, piece], x_send.at[group, c], x_recv.at[group, c], gx=right
         ).wait_recv()
         spread(group, c, lambda b: raw[group, pl.ds(pl.multiple_of(b * brick, brick), brick), :])
         both_sides(lambda side: edge_copy(side, group, c).start())
@@ -161,7 +177,10 @@
 
     first = 2 - 2 * lax.rem(gx, 2)
     second = 2 - first
+    loads[0].wait()
     loop(chunks, own_chunk)
+    for load in loads[3:]:
+        load.wait()
     loop(chunks, lambda c: far_chunk(first, c))
     loop(chunks, lambda c: apply_chunk(1, c))
     for off in range(1, n_gy):
@@ -173,7 +192,7 @@
 
     def picks(a):
         start = nb * n_gx + nb - nb * gx
-        found = [lax.rem(cols_ref[a, k] + start, nb * n_gx) for k in range(slots)]
+        found = [lax.rem(cols_ref[k, a] + start, nb * n_gx) for k in range(slots)]
         return [jnp.minimum(p, 3 * nb - 1) for p in found]
 
     def halo_copy(side, a):
@@ -199,7 +218,7 @@
                 halo_send[1, a, y - rows_y + SWEEPS] = piece.astype(bf16)
         both_sides(lambda side: halo_copy(side, a).start())
 
-    loop(nb, gradient_of)
+    unrolled(nb, gradient_of)
 
     def part_of(a):
         source = jnp.concatenate([near_app[p] for p in picks(a)], axis=0)
@@ -208,19 +227,28 @@
         ) * volume
         for k in range(slots):
             one = block[:, k * size : (k + 1) * size]
-            part[k, a] = jnp.concatenate([one[:half], one[half:]], axis=1)
-
-    loop(nb, part_of)
-
-    def part_copy(off):
+            one = jnp.concatenate([one[:half], one[half:]], axis=1)
+            part[k, a] = one
+            part_half[k, a] = one.astype(bf16)
+
+    unrolled(nb, part_of)
+
+    def part_copy(off, wide_type):
         peer = lax.rem(gy + off, n_gy)
+        source, target = (part, part_recv) if wide_type else (part_half, half_recv)
+        send, recv = (h_send, h_recv) if wide_type else (b_send, b_recv)
         return remote(
-            part.at[pl.ds(peer * own_slots, own_slots)], part_recv.at[off - 1],
-            h_send.at[off - 1], h_recv.at[off - 1], gy=peer,
-        )
-
-    for off in range(1, n_gy):
-        part_copy(off).start()
+            source.at[pl.ds(peer * own_slots, own_slots)], target.at[off - 1],
+            send.at[off - 1], recv.at[off - 1], gy=peer,
+        )
+
+    def by_distance(off, other, action):
+        apart = jnp.abs(other - gy)
+        pl.when(apart == 1)(lambda: action(off, True))
+        pl.when(apart > 1)(lambda: action(off, False))
+
+    for off in range(1, n_gy):
+        by_distance(off, lax.rem(gy + off, n_gy), lambda o, w: part_copy(o, w).start())
 
     diag = 1.0 + 2.0 / kinetic_cut
     coef = 0.5 / kinetic_cut
@@ -247,24 +275,28 @@
                     value = value * high
                 later[i] = value
             now = later
-        z_in = (z_index >= regs_ref[a, 2]) & (z_index < regs_ref[a, 3])
+        z_in = (z_index >= regs_ref[2, a]) & (z_index < regs_ref[3, a])
         base = base_of(nb + a)
         for y in range(rows_y):
             spot = gy * rows_y + y
-            y_in = jnp.where((spot >= regs_ref[a, 0]) & (spot < regs_ref[a, 1]), step_length, 0.0)
+            y_in = jnp.where((spot >= regs_ref[0, a]) & (spot < regs_ref[1, a]), step_length, 0.0)
             masked = jnp.where(z_in, now[SWEEPS + y] * y_in.astype(f32), 0.0)
             phi = wide[pl.ds(base + y, size, stride=rows_y), :]
-            out_ref[pl.ds(pl.multiple_of(a * brick, brick) + y, size, stride=rows_y), :] = phi - masked
-
-    loop(nb, finish)
-
-    for off in range(1, n_gy):
-        part_copy(off).wait_recv()
+            out_ref[pl.ds(a * brick + y, size, stride=rows_y), :] = phi - masked
+
+    unrolled(nb, finish)
+
+    mine = pl.ds(gy * own_slots, own_slots)
+
+    def take(off, wide_type):
+        part_copy(off, wide_type).wait_recv()
+        part[mine] = part[mine] + (part_recv if wide_type else half_recv)[off - 1].astype(f32)
+
+    for off in range(1, n_gy):
+        by_distance(off, lax.rem(gy + n_gy - off, n_gy), take)
     for j in range(own_slots):
         for a in range(nb):
             total = part[gy * own_slots + j, a]
-            for off in range(1, n_gy):
-                total = total + part_recv[off - 1, j, a]
             ham_ref[j, a, :half, :] = total[:, :size]
             ham_ref[j, a, half:, :] = total[:, size:]
 
@@ -278,7 +310,18 @@
     loop(nb, lambda a: both_sides(lambda side: halo_copy(side, a).wait_send()))
     for off in range(1, n_gy):
         k_copy(off).wait_send()
-        part_copy(off).wait_send()
+        by_distance(off, lax.rem(gy + off, n_gy), lambda o, w: part_copy(o, w).wait_send())
+
+
+def store_body(support_ref, ham_ref, support_out, ham_out, sem):
+    copies = [
+        pltpu.make_async_copy(support_ref, support_out, sem.at[0]),
+        pltpu.make_async_copy(ham_ref, ham_out, sem.at[1]),
+    ]
+    for copy in copies:
+        copy.start()
+    for copy in copies:
+        copy.wait()
 
 
 def local(n_gx, n_gy, support_funcs, potential, kernel, weighted, columns, regions):
@@ -288,17 +331,25 @@
     flat = orbitals * rows_y
     chunks = nb // CHUNK
     vmem = pl.BlockSpec(memory_space=pltpu.VMEM)
-    smem = pl.BlockSpec(memory_space=pltpu.SMEM)
     dma = pltpu.SemaphoreType.DMA
+    operands = (
+        columns.T, regions.T, potential, support_funcs.reshape(flat, depth), kernel, weighted
+    )
     new_support, hamiltonian = pl.pallas_call(
         functools.partial(kernel_body, n_gx, n_gy, rows_y),
         out_shape=(
             jax.ShapeDtypeStruct((flat, depth), f32),
             jax.ShapeDtypeStruct((own_slots, nb, size, size), f32),
         ),
-        in_specs=[smem, smem, vmem, vmem, vmem, vmem],
+        in_specs=[pl.BlockSpec(memory_space=pltpu.HBM)] * 6,
         out_specs=(vmem, vmem),
         scratch_shapes=[
+            pltpu.SMEM((slots, nb), jnp.int32),
+            pltpu.SMEM((4, nb), jnp.int32),
+            pltpu.VMEM((rows_y, depth), f32),
+            pltpu.VMEM((flat, depth), bf16),
+            pltpu.VMEM(kernel.shape, bf16),
+            pltpu.VMEM(kernel.shape, bf16),
             pltpu.VMEM((3, flat, depth), bf16),
             pltpu.VMEM((3 * flat, depth), f32),
             pltpu.VMEM((3 * nb, size, rows_y * depth), bf16),
@@ -311,7 +362,10 @@
             pltpu.VMEM((2, nb, SWEEPS, size, depth), bf16),
             pltpu.VMEM((2, nb, SWEEPS, size, depth), bf16),
             pltpu.VMEM((slots, nb, size // 2, 2 * size), f32),
+            pltpu.VMEM((slots, nb, size // 2, 2 * size), bf16),
             pltpu.VMEM((n_gy - 1, own_slots, nb, size // 2, 2 * size), f32),
+            pltpu.VMEM((n_gy - 1, own_slots, nb, size // 2, 2 * size), bf16),
+            dma((6,)),
             dma((3, chunks)),
             dma((3, chunks)),
             dma((2, 3 * chunks)),
@@ -323,11 +377,24 @@
             dma((2, nb)),
             dma((n_gy - 1,)),
             dma((n_gy - 1,)),
+            dma((n_gy - 1,)),
+            dma((n_gy - 1,)),
         ],
         compiler_params=pltpu.CompilerParams(
             collective_id=0, has_side_effects=True, vmem_limit_bytes=40 * 1024 * 1024
         ),
-    )(columns, regions, potential, support_funcs.reshape(flat, depth), kernel, weighted)
+    )(*[pltpu.with_memory_space_constraint(v, pltpu.HBM) for v in operands])
+    hbm = pl.BlockSpec(memory_space=pltpu.HBM)
+    new_support, hamiltonian = pl.pallas_call(
+        store_body,
+        out_shape=(
+            jax.ShapeDtypeStruct(new_support.shape, f32),
+            jax.ShapeDtypeStruct(hamiltonian.shape, f32),
+        ),
+        in_specs=[vmem, vmem],
+        out_specs=(hbm, hbm),
+        scratch_shapes=[dma((2,))],
+    )(new_support, hamiltonian)
     return (new_support.reshape(orbitals, rows_y, depth), hamiltonian)
 
 

time: 44.7 us -> 38.8 us (0.87)
  local copies, waits for them, and re-layouts: 5.8 us -> 1.56 us
  Pallas kernels: 38 us -> 36.5 us
    unnamed x14 -> x4, local copies, waits for them, and re-layouts: 5.8 us -> 1.56 us
    pallas_call x1, Pallas kernels: 38 us -> 34.4 us  [local(): pl.pallas_call(functools.partial(kernel_body, n_gx, n_gy, rows_y), out_sh...]
    pallas_call x0 -> x1, Pallas kernels: none -> 2.11 us  [local(): pl.pallas_call(store_body, out_shape=(jax.ShapeDtypeStruct(new_support.sh...]
where the time goes in v2:
time: 38.8 us; the launch traced here: 38.7 us
  Pallas kernels  36.5 us (94%)
  local copies, waits for them, and re-layouts  1.56 us (4%)
  between operations  0.65 us (2%)
    pallas_call x1, Pallas kernels, local(): pl.pallas_call(functools.partial(kernel_body, n_gx, n_gy, rows_y), out_sh...  34.4 us
    pallas_call x1, Pallas kernels, local(): pl.pallas_call(store_body, out_shape=(jax.ShapeDtypeStruct(new_support.sh...  2.11 us
    unnamed x4, local copies, waits for them, and re-layouts  1.56 us

profile of v2, /device:TPU:0, one launch (start us, length us, event | category | flops | bytes accessed | tf_op | source)
XLA Modules:
  0.0 38.7 jit_solution(17966383033261733680)
XLA Ops:
  0.6 34.4 %shard_map.77 = (f32[1536,128]{1,0:T(8,128)S(1)}, f32[1,6,64,64]{3,2,1,0:T(8,128)S(1)}) custom-call(s32[4,6]{1,0:T(4,128)} %bitcast.5, s32[4,6]{1,0:T(4,128)} %bitcast.6, f32[4,128]{1,0:T(4,128)} %pot_hbm.1, bf16[1536,128]{1,0:T(8,128)(2,1)} %bitcast.4, bf16[1,6,64,64]{3,2,1,0:T(8,128)(2,1)} %kern_hbm.1, bf16[1,6,64,64]{3,2,1,0:T(8,128)(2,1)} %wght_hbm.1), custom_call_target="tpu_custom_call" | custom-call | tf_op jit(solution)/shard_map/pallas_call | solution.py:338
  35.0 0.0 copy-start
  35.0 0.9 %copy-done = f32[1536,128]{1,0:T(8,128)} copy-done((f32[1536,128]{1,0:T(8,128)}, f32[1536,128]{1,0:T(8,128)S(1)}, u32[]{:S(2)}) %copy-start) | copy-done | bytes 786456
  35.9 0.0 copy-start.1
  35.9 0.7 %copy-done.1 = f32[1,6,64,64]{3,2,1,0:T(8,128)} copy-done((f32[1,6,64,64]{3,2,1,0:T(8,128)}, f32[1,6,64,64]{3,2,1,0:T(8,128)S(1)}, u32[]{:S(2)}) %copy-start.1) | copy-done | bytes 98328
  36.6 2.1 %shard_map.78 = (f32[1536,128]{1,0:T(8,128)}, f32[1,6,64,64]{3,2,1,0:T(8,128)}) custom-call(f32[1536,128]{1,0:T(8,128)} %copy-done, f32[1,6,64,64]{3,2,1,0:T(8,128)} %copy-done.1), custom_call_target="tpu_custom_call" | custom-call | tf_op jit(solution)/shard_map/pallas_call | solution.py:388
Async XLA Ops:
  35.0 0.9 %copy-start = (f32[1536,128]{1,0:T(8,128)}, f32[1536,128]{1,0:T(8,128)S(1)}, u32[]{:S(2)}) copy-start(f32[1536,128]{1,0:T(8,128)S(1)} %get-tuple-element.6.support_ref) | copy-start | bytes 2359300
  35.9 0.7 %copy-start.1 = (f32[1,6,64,64]{3,2,1,0:T(8,128)}, f32[1,6,64,64]{3,2,1,0:T(8,128)S(1)}, u32[]{:S(2)}) copy-start(f32[1,6,64,64]{3,2,1,0:T(8,128)S(1)} %get-tuple-element.7.ham_ref) | copy-start | bytes 294916

commit v3 on v2

--- a/solution.py
+++ b/solution.py
@@ -92,7 +92,7 @@
         x_copy(True, c).start()
         x_copy(False, c).start()
 
-    loop(chunks, start_x)
+    unrolled(chunks, start_x)
 
     def k_copy(off):
         mine = pl.ds(gy * own_slots, own_slots)
@@ -153,9 +153,10 @@
         pl.when(has_high)(lambda: edge_copy(0, group, c).wait_recv())
         for i in range(CHUNK):
             p = group * nb + c * CHUNK + i
-            base = base_of(p)
             line = [edge_recv[0, p].astype(f32)]
-            line += [wide[pl.ds(base + y, size, stride=rows_y), :] for y in range(rows_y)]
+            line += [
+                near_phi[p, :, y * depth : (y + 1) * depth].astype(f32) for y in range(rows_y)
+            ]
             line += [edge_recv[1, p].astype(f32)]
             for y in range(rows_y):
                 center = line[y + 1]
@@ -178,17 +179,21 @@
     first = 2 - 2 * lax.rem(gx, 2)
     second = 2 - first
     loads[0].wait()
-    loop(chunks, own_chunk)
+    unrolled(chunks, own_chunk)
     for load in loads[3:]:
         load.wait()
-    loop(chunks, lambda c: far_chunk(first, c))
-    loop(chunks, lambda c: apply_chunk(1, c))
+    unrolled(chunks, lambda c: far_chunk(first, c))
+    unrolled(chunks, lambda c: apply_chunk(1, c))
     for off in range(1, n_gy):
         k_copy(off).wait_recv()
     own_copy.wait()
-    loop(chunks, lambda c: far_chunk(second, c))
-    loop(chunks, lambda c: apply_chunk(first, c))
-    loop(chunks, lambda c: apply_chunk(second, c))
+
+    def interleaved(c):
+        far_chunk(second, c)
+        apply_chunk(first, c)
+
+    unrolled(chunks, interleaved)
+    unrolled(chunks, lambda c: apply_chunk(second, c))
 
     def picks(a):
         start = nb * n_gx + nb - nb * gx
@@ -276,12 +281,11 @@
                 later[i] = value
             now = later
         z_in = (z_index >= regs_ref[2, a]) & (z_index < regs_ref[3, a])
-        base = base_of(nb + a)
         for y in range(rows_y):
             spot = gy * rows_y + y
             y_in = jnp.where((spot >= regs_ref[0, a]) & (spot < regs_ref[1, a]), step_length, 0.0)
             masked = jnp.where(z_in, now[SWEEPS + y] * y_in.astype(f32), 0.0)
-            phi = wide[pl.ds(base + y, size, stride=rows_y), :]
+            phi = near_phi[nb + a, :, y * depth : (y + 1) * depth].astype(f32)
             out_ref[pl.ds(a * brick + y, size, stride=rows_y), :] = phi - masked
 
     unrolled(nb, finish)
@@ -394,6 +398,7 @@
         in_specs=[vmem, vmem],
         out_specs=(hbm, hbm),
         scratch_shapes=[dma((2,))],
+        compiler_params=pltpu.CompilerParams(vmem_limit_bytes=8 * 1024 * 1024),
     )(new_support, hamiltonian)
     return (new_support.reshape(orbitals, rows_y, depth), hamiltonian)
 

time: 38.8 us -> 36 us (0.928)
  local copies, waits for them, and re-layouts: 1.56 us -> 0 us
  Pallas kernels: 36.5 us -> 35.2 us
    unnamed x4 -> x0, local copies, waits for them, and re-layouts: 1.56 us -> none
    pallas_call x1, Pallas kernels: 2.11 us -> 0.96 us  [local(): pl.pallas_call(store_body, out_shape=(jax.ShapeDtypeStruct(new_support.sh...]
where the time goes in v3:
time: 36 us; the launch traced here: 35.9 us
  Pallas kernels  35.2 us (98%)
  between operations  0.64 us (2%)
    pallas_call x1, Pallas kernels, local(): pl.pallas_call(functools.partial(kernel_body, n_gx, n_gy, rows_y), out_sh...  34.3 us
    pallas_call x1, Pallas kernels, local(): pl.pallas_call(store_body, out_shape=(jax.ShapeDtypeStruct(new_support.sh...  0.96 us

profile of v3, /device:TPU:0, one launch (start us, length us, event | category | flops | bytes accessed | tf_op | source)
XLA Modules:
  0.0 35.9 jit_solution(16598925868666734234)
XLA Ops:
  0.6 34.3 %shard_map.77 = (f32[1536,128]{1,0:T(8,128)S(1)}, f32[1,6,64,64]{3,2,1,0:T(8,128)S(1)}) custom-call(s32[4,6]{1,0:T(4,128)} %bitcast.5, s32[4,6]{1,0:T(4,128)} %bitcast.6, f32[4,128]{1,0:T(4,128)} %pot_hbm.1, bf16[1536,128]{1,0:T(8,128)(2,1)} %bitcast.4, bf16[1,6,64,64]{3,2,1,0:T(8,128)(2,1)} %kern_hbm.1, bf16[1,6,64,64]{3,2,1,0:T(8,128)(2,1)} %wght_hbm.1), custom_call_target="tpu_custom_call" | custom-call | tf_op jit(solution)/shard_map/pallas_call | solution.py:342
  34.9 1.0 %shard_map.78 = (f32[1536,128]{1,0:T(8,128)}, f32[1,6,64,64]{3,2,1,0:T(8,128)}) custom-call(f32[1536,128]{1,0:T(8,128)S(1)} %get-tuple-element.6.support_ref, f32[1,6,64,64]{3,2,1,0:T(8,128)S(1)} %get-tuple-element.7.ham_ref), custom_call_target="tpu_custom_call" | custom-call | tf_op jit(solution)/shard_map/pallas_call | solution.py:392

commit v4 on v3

--- a/solution.py
+++ b/solution.py
@@ -94,14 +94,29 @@
 
     unrolled(chunks, start_x)
 
-    def k_copy(off):
-        mine = pl.ds(gy * own_slots, own_slots)
+    def k_copy(up, d):
+        origin = gy - (d - 1) if up else gy + (d - 1)
+        place = pl.ds(jnp.clip(origin, 0, n_gy - 1) * own_slots, own_slots)
+        side = 0 if up else 1
         return remote(
-            pack, packs.at[mine], k_send.at[off - 1], k_recv.at[off - 1], gy=lax.rem(gy + off, n_gy)
-        )
-
-    for off in range(1, n_gy):
-        k_copy(off).start()
+            pack if d == 1 else packs.at[place], packs.at[place],
+            k_send.at[side, d - 1], k_recv.at[side, d - 1],
+            gy=jnp.minimum(gy + 1, n_gy - 1) if up else jnp.maximum(gy - 1, 0),
+        )
+
+    def k_sends(d, action):
+        pl.when((gy - (d - 1) >= 0) & has_high)(lambda: action(k_copy(True, d)))
+        pl.when((gy + (d - 1) < n_gy) & has_low)(lambda: action(k_copy(False, d)))
+
+    def k_arrived(d):
+        pl.when(gy - d >= 0)(lambda: k_copy(True, d).wait_recv())
+        pl.when(gy + d < n_gy)(lambda: k_copy(False, d).wait_recv())
+
+    def k_relay(d):
+        k_arrived(d - 1)
+        k_sends(d, lambda copy: copy.start())
+
+    k_sends(1, lambda copy: copy.start())
     own_copy = pltpu.make_async_copy(pack, packs.at[pl.ds(gy * own_slots, own_slots)], k_own)
     own_copy.start()
 
@@ -183,9 +198,11 @@
     for load in loads[3:]:
         load.wait()
     unrolled(chunks, lambda c: far_chunk(first, c))
+    if n_gy > 2:
+        k_relay(2)
     unrolled(chunks, lambda c: apply_chunk(1, c))
-    for off in range(1, n_gy):
-        k_copy(off).wait_recv()
+    for d in range(3, n_gy):
+        k_relay(d)
     own_copy.wait()
 
     def interleaved(c):
@@ -194,6 +211,7 @@
 
     unrolled(chunks, interleaved)
     unrolled(chunks, lambda c: apply_chunk(second, c))
+    k_arrived(n_gy - 1)
 
     def picks(a):
         start = nb * n_gx + nb - nb * gx
@@ -313,7 +331,7 @@
         loop(chunks, lambda c: both_sides(lambda side: edge_copy(side, group, c).wait_send()))
     loop(nb, lambda a: both_sides(lambda side: halo_copy(side, a).wait_send()))
     for off in range(1, n_gy):
-        k_copy(off).wait_send()
+        k_sends(off, lambda copy: copy.wait_send())
         by_distance(off, lax.rem(gy + off, n_gy), lambda o, w: part_copy(o, w).wait_send())
 
 
@@ -374,8 +392,8 @@
             dma((3, chunks)),
             dma((2, 3 * chunks)),
             dma((2, 3 * chunks)),
-            dma((n_gy - 1,)),
-            dma((n_gy - 1,)),
+            dma((2, n_gy - 1)),
+            dma((2, n_gy - 1)),
             dma(()),
             dma((2, nb)),
             dma((2, nb)),

time: 36 us -> 34.4 us (0.956)
  Pallas kernels: 35.2 us -> 33.6 us
    pallas_call x1, Pallas kernels: 34.3 us -> 32.7 us  [local(): pl.pallas_call(functools.partial(kernel_body, n_gx, n_gy, rows_y), out_sh...]
where the time goes in v4:
time: 34.4 us; the launch traced here: 34.3 us
  Pallas kernels  33.6 us (98%)
  between operations  0.64 us (2%)
    pallas_call x1, Pallas kernels, local(): pl.pallas_call(functools.partial(kernel_body, n_gx, n_gy, rows_y), out_sh...  32.7 us
    pallas_call x1, Pallas kernels, local(): pl.pallas_call(store_body, out_shape=(jax.ShapeDtypeStruct(new_support.sh...  0.96 us

profile of v4, /device:TPU:0, one launch (start us, length us, event | category | flops | bytes accessed | tf_op | source)
XLA Modules:
  0.0 34.3 jit_solution(172674557656685186)
XLA Ops:
  0.6 32.7 %shard_map.77 = (f32[1536,128]{1,0:T(8,128)S(1)}, f32[1,6,64,64]{3,2,1,0:T(8,128)S(1)}) custom-call(s32[4,6]{1,0:T(4,128)} %bitcast.5, s32[4,6]{1,0:T(4,128)} %bitcast.6, f32[4,128]{1,0:T(4,128)} %pot_hbm.1, bf16[1536,128]{1,0:T(8,128)(2,1)} %bitcast.4, bf16[1,6,64,64]{3,2,1,0:T(8,128)(2,1)} %kern_hbm.1, bf16[1,6,64,64]{3,2,1,0:T(8,128)(2,1)} %wght_hbm.1), custom_call_target="tpu_custom_call" | custom-call | tf_op jit(solution)/shard_map/pallas_call | solution.py:360
  33.3 1.0 %shard_map.78 = (f32[1536,128]{1,0:T(8,128)}, f32[1,6,64,64]{3,2,1,0:T(8,128)}) custom-call(f32[1536,128]{1,0:T(8,128)S(1)} %get-tuple-element.6.support_ref, f32[1,6,64,64]{3,2,1,0:T(8,128)S(1)} %get-tuple-element.7.ham_ref), custom_call_target="tpu_custom_call" | custom-call | tf_op jit(solution)/shard_map/pallas_call | solution.py:410
